TPU v7x, 32 devices: a whole 2x2x4 slice. The times are simulated.
32 devices in a mesh: dp: 2 (over y), seq: 4 (over z), tensor: 4 (over x, core).
Axes of the slice: x: 2, y: 2, z: 4, core: 2. Of those that a mesh axis runs over, the one named last changes fastest.
Arguments:
- layer_input: bfloat16 [6, 1024, 2048], P('dp', 'seq'), may hold values from -6 to 6
- lengths: int32 [6], P('dp'), may hold values from 256 to 1024, as said below
- cotangent: bfloat16 [6, 1024, 2048], P('dp', ('seq', 'tensor')), may hold values from -6 to 6
- ln1_gain: bfloat16 [2048], replicated, may hold values from 0.5 to 1.5
- ln1_bias: bfloat16 [2048], replicated, may hold values from -3 to 3
- w_query: bfloat16 [2048, 2048], P(None, 'tensor'), may hold values from -0.125 to 0.125
- b_query: bfloat16 [2048], P('tensor'), may hold values from -3 to 3
- w_kv: bfloat16 [2048, 256], replicated, may hold values from -0.125 to 0.125
- b_value: bfloat16 [128], replicated, may hold values from -3 to 3
- w_out: bfloat16 [2048, 2048], P('tensor'), may hold values from -0.5 to 0.5
- b_out: bfloat16 [2048], replicated, may hold values from -3 to 3
- ln2_gain: bfloat16 [2048], replicated, may hold values from 0.5 to 1.5
- ln2_bias: bfloat16 [2048], replicated, may hold values from -3 to 3
- w_up: bfloat16 [2048, 8192], P(None, 'tensor'), may hold values from -0.125 to 0.125
- b_up: bfloat16 [8192], P('tensor'), may hold values from -3 to 3
- w_down: bfloat16 [8192, 2048], P('tensor'), may hold values from -0.0625 to 0.0625
- b_down: bfloat16 [2048], replicated, may hold values from -3 to 3
Outputs:
- layer_output: bfloat16 [6, 1024, 2048], P('dp', ('seq', 'tensor'))
- input_grad: float32 [6, 1024, 2048], P('dp', ('seq', 'tensor'))
- g_w_query: float32 [2048, 2048], P(('dp', 'seq'), 'tensor')
- g_b_query: float32 [16, 128], P('tensor', ('dp', 'seq'))
- g_w_kv: float32 [2048, 256], P(('dp', 'seq', 'tensor'))
- g_b_value: float32 [128], P(('dp', 'seq', 'tensor'))
- g_w_out: float32 [2048, 2048], P('tensor', ('dp', 'seq'))
- g_w_up: float32 [2048, 8192], P(('dp', 'seq'), 'tensor')
- g_b_up: float32 [64, 128], P('tensor', ('dp', 'seq'))
- g_w_down: float32 [8192, 2048], P('tensor', ('dp', 'seq'))
- g_norms_biases: float32 [6, 2048], P(None, ('dp', 'seq', 'tensor'))
Inputs may be any that keep to these rules, and one draw needn't show every extreme that they name: `lengths`: the number of real tokens at the start of each row; the rest of the row is padding.
All inputs are finite; a program needn't handle non-finite values.
Results may differ from a plain program's by a relative error of at most 0.012.
Values may be sent and summed in bfloat16 or wider, within the bound.
A program may use at most 256 MiB of HBM per device.

v0:
```python
import math
import jax
import jax.numpy as jnp
from jax import lax
from jax.sharding import PartitionSpec as P

NORM_EPS = 1e-05


def normalize(values_in):
    row_mean = jnp.mean(values_in, -1, keepdims=True)
    centered = values_in - row_mean
    variance = jnp.mean(centered * centered, -1, keepdims=True)
    inv_std = lax.rsqrt(variance + NORM_EPS)
    return (centered * inv_std, inv_std)


def norm_back(grad_in, normed, inv_std, norm_gain):
    scaled = grad_in * norm_gain
    mean_scaled = jnp.mean(scaled, -1, keepdims=True)
    mean_mixed = jnp.mean(scaled * normed, -1, keepdims=True)
    return inv_std * (scaled - mean_scaled - normed * mean_mixed)


def across_rows(left_in, right_in):
    return lax.dot_general(
        left_in, right_in, (((0,), (0,)), ((), ())), preferred_element_type=jnp.float32
    )


def times_transposed(left_in, right_in):
    return lax.dot_general(
        left_in, right_in, (((1,), (1,)), ((), ())), preferred_element_type=jnp.float32
    )


def shards(
    layer_input,
    lengths,
    cotangent,
    ln1_gain,
    ln1_bias,
    w_query,
    b_query,
    w_kv,
    b_value,
    w_out,
    b_out,
    ln2_gain,
    ln2_bias,
    w_up,
    b_up,
    w_down,
    b_down,
):
    n_rows, seq_len, model_width = layer_input.shape
    share_len = seq_len // lax.axis_size("tensor")
    tensor_index = lax.axis_index("tensor")
    seq_index = lax.axis_index("seq")
    full_len = seq_len * lax.axis_size("seq")
    head_size = w_kv.shape[1] // 2
    num_heads = w_query.shape[1] // head_size
    q_scale = 1.0 / math.sqrt(head_size)

    def own_rows(values_in):
        return lax.dynamic_slice_in_dim(values_in, tensor_index * share_len, share_len, 1)

    positions = seq_index * seq_len + jnp.arange(seq_len, dtype=jnp.int32)
    key_places = jnp.arange(full_len, dtype=jnp.int32)
    is_valid = (positions[None, :] < lengths[:, None]).astype(jnp.float32)
    allowed_keys = (key_places[None, None, :] <= positions[None, :, None]) & (
        key_places[None, None, :] < lengths[:, None, None]
    )
    valid_own = own_rows(is_valid)
    x_float = layer_input.astype(jnp.float32)
    normed_x1, inv_one = normalize(x_float)
    normed_one = (normed_x1 * ln1_gain + ln1_bias).astype(jnp.bfloat16)
    flat_one = normed_one.reshape(n_rows * seq_len, model_width)
    queries = (
        (jnp.dot(flat_one, w_query, preferred_element_type=jnp.float32) + b_query) * q_scale
    ).astype(jnp.bfloat16)
    queries = queries.reshape(n_rows, seq_len, num_heads, head_size)
    kv_bias = jnp.concatenate([jnp.zeros((head_size,), jnp.float32), b_value.astype(jnp.float32)])
    kv_local = (jnp.dot(flat_one, w_kv, preferred_element_type=jnp.float32) + kv_bias).astype(
        jnp.bfloat16
    )
    kv_local = kv_local.reshape(n_rows, seq_len, 2 * head_size)
    kv_all = lax.all_gather(kv_local, "seq", axis=1, tiled=True)
    key_rows = kv_all[..., :head_size]
    value_rows = kv_all[..., head_size:]

    def scores_of(query_rows):
        raw_scores = jnp.einsum(
            "rshd,rld->rhsl", query_rows, key_rows, preferred_element_type=jnp.float32
        )
        return jnp.where(allowed_keys[:, None], raw_scores, -1e30)

    scores = scores_of(queries)
    row_max = jnp.max(scores, -1, keepdims=True)
    exp_scores = jnp.exp(scores - row_max)
    exp_total = jnp.sum(exp_scores, -1, keepdims=True)
    soft_probs = exp_scores / exp_total
    log_total = row_max + jnp.log(exp_total)
    mixed_heads = jnp.einsum(
        "rhsl,rld->rshd",
        soft_probs.astype(jnp.bfloat16),
        value_rows,
        preferred_element_type=jnp.float32,
    ).astype(jnp.bfloat16)
    mixed_heads = mixed_heads.reshape(n_rows * seq_len, num_heads * head_size)
    attn_part = jnp.dot(mixed_heads, w_out, preferred_element_type=jnp.float32).reshape(
        n_rows, seq_len, model_width
    )
    residual = x_float + (lax.psum(attn_part, "tensor") + b_out)
    normed_x2, inv_two = normalize(residual)
    normed_two = (normed_x2 * ln2_gain + ln2_bias).astype(jnp.bfloat16)
    resid_own = own_rows(residual)
    normed_x2_own = own_rows(normed_x2)
    flat_two = normed_two.reshape(n_rows * seq_len, model_width)
    pre_act = jnp.dot(flat_two, w_up, preferred_element_type=jnp.float32) + b_up
    activated, gelu_pull = jax.vjp(
        lambda inner_in: jax.nn.gelu(inner_in, approximate=True), pre_act
    )
    act_low = activated.astype(jnp.bfloat16)
    mlp_part = jnp.dot(act_low, w_down, preferred_element_type=jnp.float32).reshape(
        n_rows, seq_len, model_width
    )
    mlp_own = (
        lax.psum_scatter(
            mlp_part.astype(jnp.bfloat16), "tensor", scatter_dimension=1, tiled=True
        ).astype(jnp.float32)
        + b_down
    )
    y_own = (valid_own[..., None] * (resid_own + mlp_own)).astype(jnp.bfloat16)
    cot_full = lax.all_gather(cotangent, "tensor", axis=1, tiled=True)
    grad_y = cot_full.astype(jnp.float32) * is_valid[..., None]
    grad_y_low = grad_y.astype(jnp.bfloat16).reshape(n_rows * seq_len, model_width)
    grad_y_own = cotangent.astype(jnp.float32) * valid_own[..., None]
    g_w_down = across_rows(act_low, grad_y_low)
    grad_act = times_transposed(grad_y_low, w_down)
    grad_pre = gelu_pull(grad_act)[0].astype(jnp.bfloat16)
    g_w_up = across_rows(flat_two, grad_pre)
    g_b_up = jnp.sum(grad_pre.astype(jnp.float32), axis=0)
    grad_a2 = times_transposed(grad_pre, w_up).reshape(n_rows, seq_len, model_width)
    grad_n2 = lax.psum(grad_a2, "tensor")
    grad_resid = grad_y + norm_back(grad_n2, normed_x2, inv_two, ln2_gain)
    grad_resid_low = grad_resid.astype(jnp.bfloat16)
    grad_resid_own = own_rows(grad_resid)
    grad_n2_own = own_rows(grad_n2)
    grad_resid_own_low = own_rows(grad_resid_low)
    g_ln2_gain = jnp.sum(grad_n2_own * normed_x2_own, axis=(0, 1))
    g_ln2_bias = jnp.sum(grad_n2_own, axis=(0, 1))
    g_b_out = jnp.sum(grad_resid_own_low.astype(jnp.float32), axis=(0, 1))
    g_b_down = jnp.sum(grad_y_own, axis=(0, 1))
    flat_resid = grad_resid_low.reshape(n_rows * seq_len, model_width)
    g_w_out = across_rows(mixed_heads, flat_resid)
    grad_mixed = times_transposed(flat_resid, w_out).astype(jnp.bfloat16)
    grad_mixed = grad_mixed.reshape(n_rows, seq_len, num_heads, head_size)
    again_probs = jnp.exp(scores_of(queries) - log_total)
    grad_probs = jnp.einsum(
        "rshd,rld->rhsl", grad_mixed, value_rows, preferred_element_type=jnp.float32
    )
    inner_sum = jnp.sum(again_probs * grad_probs, -1, keepdims=True)
    grad_scores = (again_probs * (grad_probs - inner_sum)).astype(jnp.bfloat16)
    grad_query = jnp.einsum(
        "rhsl,rld->rshd", grad_scores, key_rows, preferred_element_type=jnp.float32
    ).astype(jnp.bfloat16)
    grad_keys = jnp.einsum(
        "rhsl,rshd->rld", grad_scores, queries, preferred_element_type=jnp.float32
    )
    grad_values = jnp.einsum(
        "rhsl,rshd->rld",
        again_probs.astype(jnp.bfloat16),
        grad_mixed,
        preferred_element_type=jnp.float32,
    )
    grad_kv = jnp.concatenate([grad_keys, grad_values], -1)
    grad_kv_own = lax.psum_scatter(
        grad_kv, ("seq", "tensor"), scatter_dimension=1, tiled=True
    ).astype(jnp.bfloat16)
    flat_query = grad_query.reshape(n_rows * seq_len, num_heads * head_size)
    g_w_query = across_rows(flat_one, flat_query) * q_scale
    g_b_query = jnp.sum(flat_query.astype(jnp.float32), axis=0) * q_scale
    grad_n1_part = (times_transposed(flat_query, w_query) * q_scale).reshape(
        n_rows, seq_len, model_width
    )
    grad_n1_own = lax.psum_scatter(
        grad_n1_part.astype(jnp.bfloat16), "tensor", scatter_dimension=1, tiled=True
    ).astype(jnp.float32)
    flat_kv = grad_kv_own.reshape(n_rows * share_len, 2 * head_size)
    grad_n1_own = grad_n1_own + times_transposed(flat_kv, w_kv).reshape(
        n_rows, share_len, model_width
    )
    one_own = own_rows(normed_one).reshape(n_rows * share_len, model_width)
    g_w_kv = across_rows(one_own, flat_kv)
    g_b_value = jnp.sum(flat_kv[:, head_size:].astype(jnp.float32), axis=0)
    normed_x1_own = own_rows(normed_x1)
    x_grad_own = grad_resid_own + norm_back(grad_n1_own, normed_x1_own, own_rows(inv_one), ln1_gain)
    g_ln1_gain = jnp.sum(grad_n1_own * normed_x1_own, axis=(0, 1))
    g_ln1_bias = jnp.sum(grad_n1_own, axis=(0, 1))
    query_table = g_b_query.reshape(num_heads, head_size)
    up_table = g_b_up.reshape(-1, 128)
    summed = (
        lax.psum_scatter(g_w_query, ("dp", "seq"), scatter_dimension=0, tiled=True),
        lax.psum_scatter(query_table, ("dp", "seq"), scatter_dimension=1, tiled=True),
        lax.psum_scatter(g_w_out, ("dp", "seq"), scatter_dimension=1, tiled=True),
        lax.psum_scatter(g_w_up, ("dp", "seq"), scatter_dimension=0, tiled=True),
        lax.psum_scatter(up_table, ("dp", "seq"), scatter_dimension=1, tiled=True),
        lax.psum_scatter(g_w_down, ("dp", "seq"), scatter_dimension=1, tiled=True),
    )
    small_grads = jnp.stack([g_ln1_gain, g_ln1_bias, g_ln2_gain, g_ln2_bias, g_b_out, g_b_down])
    shared = (
        lax.psum_scatter(g_w_kv, ("dp", "seq", "tensor"), scatter_dimension=0, tiled=True),
        lax.psum_scatter(small_grads, ("dp", "seq", "tensor"), scatter_dimension=1, tiled=True),
        lax.psum_scatter(g_b_value, ("dp", "seq", "tensor"), scatter_dimension=0, tiled=True),
    )
    return (
        y_own,
        x_grad_own,
        summed[0],
        summed[1],
        shared[0],
        shared[2],
        summed[2],
        summed[3],
        summed[4],
        summed[5],
        shared[1],
    )


def solution(mesh):
    placed = (
        P("dp", "seq", None),
        P("dp"),
        P("dp", ("seq", "tensor"), None),
        P(),
        P(),
        P(None, "tensor"),
        P("tensor"),
        P(),
        P(),
        P("tensor", None),
        P(),
        P(),
        P(),
        P(None, "tensor"),
        P("tensor"),
        P("tensor", None),
        P(),
    )
    return jax.shard_map(
        shards,
        mesh=mesh,
        in_specs=placed,
        out_specs=(
            P("dp", ("seq", "tensor"), None),
            P("dp", ("seq", "tensor"), None),
            P(("dp", "seq"), "tensor"),
            P("tensor", ("dp", "seq")),
            P(("dp", "seq", "tensor"), None),
            P(("dp", "seq", "tensor")),
            P("tensor", ("dp", "seq")),
            P(("dp", "seq"), "tensor"),
            P("tensor", ("dp", "seq")),
            P("tensor", ("dp", "seq")),
            P(None, ("dp", "seq", "tensor")),
        ),
        check_vma=False,
    )
```

profile of v0, /device:TPU:0, one launch (start us, length us, event | category | flops | bytes accessed | tf_op | source)
XLA Modules:
  0.0 1648.8 jit_solution(9399819819224728491)
XLA Ops:
  30.5 29.8 %all-gather.3.cloned.1.call-done = bf16[3,1024,256]{2,1,0:T(8,128)(2,1)} async-done(((bf16[3,256,256]{2,1,0:T(8,128)(2,1)}), bf16[3,1024,256]{2,1,0:T(8,128)(2,1)}) %all-gather.3.cloned.1.call-update) | async-done | bytes 1572880 | tf_op jit(solution)/shard_map/all_gather | solution.py:88
  60.4 7.9 fusion.4
  68.3 7.4 fusion.3
  75.8 6.5 fusion.28
  93.4 117.9 %all-reduce.7.cloned.1.call-done = f32[3,256,2048]{2,1,0:T(8,128)} async-done(((f32[3,256,2048]{2,1,0:T(8,128)}), f32[3,256,2048]{2,1,0:T(8,128)}) %all-reduce.7.cloned.1.call-update) | async-done | bytes 6291472 | tf_op jit(solution)/shard_map/psum | solution.py:114
  224.9 8.5 fusion.49
  233.4 14.9 convert_reduce_fusion.1
  248.3 8.6 fusion.50
  257.0 13.3 convolution_convert_fusion
  270.3 106.6 %all-reduce.9.cloned.1.call-done = f32[3,256,2048]{2,1,0:T(8,128)} async-done(((f32[3,256,2048]{2,1,0:T(8,128)}), f32[3,256,2048]{2,1,0:T(8,128)}) %all-reduce.9.cloned.1.call-update) | async-done | bytes 6291472 | tf_op jit(solution)/shard_map/psum | solution.py:145
  384.2 6.1 fusion.47
  399.3 8.6 fusion
  407.9 6.7 fusion.2
  429.4 9.6 fusion.25
  454.8 98.2 %all-reduce.10 = bf16[3,1024,256]{2,0,1:T(4,128)(2,1)} all-reduce(f32[3,1024,256]{2,0,1:T(4,128)} %copy.69), channel_id=4, replica_groups=mesh['dp'=2,'seq'=4,'tensor'=4] {'seq','tensor'}, use_global_device_ids=true, to_apply=%region_13.14.clone | all-reduce | flops 786432 | bytes 4718592
  582.3 13.9 fusion.45
  596.3 12.5 fusion.51
  611.0 40.6 %all-reduce.2 = f32[128]{0:T(128)S(1)} all-reduce(f32[128]{0:T(128)S(1)} %convert_reduce_fusion.4), channel_id=8, replica_groups=mesh['dp'=2,'seq'=4,'tensor'=4] {'dp','seq','tensor'}, use_global_device_ids=true, to_apply=%region_21.22.clone | all-reduce | flops 128 | bytes 1024
  657.5 99.5 %reduce-scatter.35.cloned.1.call-done = f32[64,6]{1,0:T(8,128)} async-done(((f32[2048,6]{1,0:T(8,128)}), f32[64,6]{1,0:T(8,128)}) %reduce-scatter.35.cloned.1.call-update) | async-done | bytes 1552
  758.4 135.5 %reduce-scatter.23.cloned.1.call-done = f32[64,256]{1,0:T(8,128)} async-done(((f32[2048,256]{1,0:T(8,128)}), f32[64,256]{1,0:T(8,128)}) %reduce-scatter.23.cloned.1.call-update) | async-done | bytes 65552 | tf_op jit(solution)/shard_map/reduce_scatter | solution.py:213
  893.9 89.4 %reduce-scatter.25.cloned.1.call-done = f32[512,256]{1,0:T(8,128)} async-done(((f32[512,2048]{1,0:T(8,128)}), f32[512,256]{1,0:T(8,128)}) %reduce-scatter.25.cloned.1.call-update) | async-done | bytes 524304 | tf_op jit(solution)/shard_map/reduce_scatter | solution.py:206
  983.4 92.0 %reduce-scatter.21.cloned.1.call-done = f32[256,512]{1,0:T(8,128)} async-done(((f32[2048,512]{1,0:T(8,128)}), f32[256,512]{1,0:T(8,128)}) %reduce-scatter.21.cloned.1.call-update) | async-done | bytes 524304 | tf_op jit(solution)/shard_map/reduce_scatter | solution.py:204
  1075.4 283.5 %reduce-scatter.29.cloned.1.call-done = f32[2048,256]{1,0:T(8,128)} async-done(((f32[2048,2048]{1,0:T(8,128)}), f32[2048,256]{1,0:T(8,128)}) %reduce-scatter.29.cloned.1.call-update) | async-done | bytes 2097168 | tf_op jit(solution)/shard_map/reduce_scatter | solution.py:209
  1358.9 282.9 %reduce-scatter.27.cloned.1.call-done = f32[256,2048]{1,0:T(8,128)} async-done(((f32[2048,2048]{1,0:T(8,128)}), f32[256,2048]{1,0:T(8,128)}) %reduce-scatter.27.cloned.1.call-update) | async-done | bytes 2097168 | tf_op jit(solution)/shard_map/reduce_scatter | solution.py:207
  (172 shorter events, 132.6 us)
Async XLA Ops:
  7.2 76.0 %copy-start = (bf16[512,2048]{1,0:T(8,128)(2,1)S(1)}, bf16[512,2048]{1,0:T(8,128)(2,1)}, u32[]{:S(2)}) copy-start(bf16[512,2048]{1,0:T(8,128)(2,1)} %param.26) | copy-start | bytes 6291460
  7.2 53.2 %all-gather.3.cloned.1.call-start = ((), (), s32[]{:S(2)}) async-start(), calls=%async_computation.10 | async-start | bytes 1966080 | tf_op jit(solution)/shard_map/all_gather | solution.py:88
  20.5 68.9 %all-gather.5.cloned.1.call-start = ((), (), s32[]{:S(2)}) async-start(), calls=%async_computation.13 | async-start | bytes 3932160 | tf_op jit(solution)/shard_map/all_gather | solution.py:135
  21.2 190.1 %all-reduce.7.cloned.1.call-start = ((), (), s32[]{:S(2)}) async-start(), calls=%async_computation.11 | async-start | bytes 12582912 | tf_op jit(solution)/shard_map/psum | solution.py:114
  21.5 8.2 copy-start.29
  87.7 289.2 %all-reduce.9.cloned.1.call-start = ((), (), s32[]{:S(2)}) async-start(), calls=%async_computation.14 | async-start | bytes 12582912 | tf_op jit(solution)/shard_map/psum | solution.py:145
  222.1 11.3 copy-start.14
  224.9 8.5 copy-start.13
  248.3 8.6 copy-start.32
  256.9 300.6 %reduce-scatter.17.cloned.1.call-start = ((), (), s32[]{:S(2)}) async-start(), calls=%async_computation.12 | async-start | bytes 3932160 | tf_op jit(solution)/shard_map/reduce_scatter | solution.py:129
  270.2 290.2 %reduce-scatter.19.cloned.1.call-start = ((), (), s32[]{:S(2)}) async-start(), calls=%async_computation.15 | async-start | bytes 3932160 | tf_op jit(solution)/shard_map/reduce_scatter | solution.py:187
  407.9 9.5 copy-start.10
  426.9 182.6 %reduce-scatter.33.cloned.1.call-start = ((), (), s32[]{:S(2)}) async-start(), calls=%async_computation.22 | async-start | bytes 73728
  429.1 223.1 %reduce-scatter.31.cloned.1.call-start = ((), (), s32[]{:S(2)}) async-start(), calls=%async_computation.21 | async-start | bytes 73728
  429.4 9.6 copy-start.7
  454.8 102.7 %copy-start.15 = (bf16[3,64,2048]{2,1,0:T(8,128)(2,1)S(1)}, bf16[3,64,2048]{2,1,0:T(8,128)(2,1)}, u32[]{:S(2)}) copy-start(bf16[3,64,2048]{2,1,0:T(8,128)(2,1)} %param.19) | copy-start | bytes 2359300
  454.8 105.7 %copy-start.19 = (f32[2048]{0:T(1024)S(1)}, f32[2048]{0:T(1024)}, u32[]{:S(2)}) copy-start(f32[2048]{0:T(1024)} %copy-done.18) | copy-start | bytes 24580
  555.3 201.7 %reduce-scatter.35.cloned.1.call-start = ((), (), s32[]{:S(2)}) async-start(), calls=%async_computation.23 | async-start | bytes 1081344
  560.5 8.4 copy-start.12
  565.8 328.1 %reduce-scatter.23.cloned.1.call-start = ((), (), s32[]{:S(2)}) async-start(), calls=%async_computation.17 | async-start | bytes 2162688 | tf_op jit(solution)/shard_map/reduce_scatter | solution.py:213
  568.8 414.5 %reduce-scatter.25.cloned.1.call-start = ((), (), s32[]{:S(2)}) async-start(), calls=%async_computation.18 | async-start | bytes 4718592 | tf_op jit(solution)/shard_map/reduce_scatter | solution.py:206
  576.2 499.1 %reduce-scatter.21.cloned.1.call-start = ((), (), s32[]{:S(2)}) async-start(), calls=%async_computation.16 | async-start | bytes 4718592 | tf_op jit(solution)/shard_map/reduce_scatter | solution.py:204
  582.0 776.9 %reduce-scatter.29.cloned.1.call-start = ((), (), s32[]{:S(2)}) async-start(), calls=%async_computation.20 | async-start | bytes 18874368 | tf_op jit(solution)/shard_map/reduce_scatter | solution.py:209
  596.2 1045.5 %reduce-scatter.27.cloned.1.call-start = ((), (), s32[]{:S(2)}) async-start(), calls=%async_computation.19 | async-start | bytes 18874368 | tf_op jit(solution)/shard_map/reduce_scatter | solution.py:207
  (25 other events, 120.0 us)
Sparse Core Ops, SparseCore 0:
  20.6 39.7 all-gather.2
  61.9 27.3 all-gather.4
  91.7 119.5 all-reduce.6
  257.0 119.7 all-reduce.8
  379.2 37.9 reduce-scatter.16
  427.1 42.3 reduce-scatter.18
  472.9 66.0 reduce-scatter.32
  555.4 63.4 reduce-scatter.30
  621.2 135.7 reduce-scatter.34
  759.7 134.2 reduce-scatter.22
  898.2 85.1 reduce-scatter.24
  987.4 87.9 reduce-scatter.20
  1079.7 279.1 reduce-scatter.28
  1363.1 278.6 reduce-scatter.26
where the time goes:
time: 1650 us
  waiting for transfers between devices  1240 us (75%)
  matrix products  150 us (9%)
  blocking collectives  139 us (8%)
  other arithmetic  64.6 us (4%)
  local copies, waits for them, and re-layouts  38.7 us (2%)
    reduce_scatter x1, waiting for transfers between devices, shards(): lax.psum_scatter(g_w_down, ('dp', 'seq'), scatter_dimension=1, tiled=True)  284 us
    reduce_scatter x1, waiting for transfers between devices, shards(): lax.psum_scatter(g_w_up, ('dp', 'seq'), scatter_dimension=0, tiled=True)  283 us
    unnamed x2, blocking collectives  139 us
    reduce_scatter x1, waiting for transfers between devices, shards(): lax.psum_scatter(g_w_kv, ('dp', 'seq', 'tensor'), scatter_dimension=0, ti...  136 us
    psum x1, waiting for transfers between devices, shards(): residual = x_float + (lax.psum(attn_part, 'tensor') + b_out)  118 us
    psum x1, waiting for transfers between devices, shards(): grad_n2 = lax.psum(grad_a2, 'tensor')  107 us
    unnamed x17, waiting for transfers between devices  100 us
    reduce_scatter x1, waiting for transfers between devices, shards(): lax.psum_scatter(g_w_query, ('dp', 'seq'), scatter_dimension=0, tiled=True)  92 us
  transfers between devices with their start and end apart: 14, of which 10 were waited for; matrix products, arithmetic and copies ran while one was open for 11% of the time, Pallas kernels for 0%

commit v1 on v0

--- a/solution.py
+++ b/solution.py
@@ -142,7 +142,7 @@
     g_w_up = across_rows(flat_two, grad_pre)
     g_b_up = jnp.sum(grad_pre.astype(jnp.float32), axis=0)
     grad_a2 = times_transposed(grad_pre, w_up).reshape(n_rows, seq_len, model_width)
-    grad_n2 = lax.psum(grad_a2, "tensor")
+    grad_n2 = jnp.sum(lax.all_gather(grad_a2, "tensor"), axis=0)
     grad_resid = grad_y + norm_back(grad_n2, normed_x2, inv_two, ln2_gain)
     grad_resid_low = grad_resid.astype(jnp.bfloat16)
     grad_resid_own = own_rows(grad_resid)

time: 1650 us -> 1700 us (1.030)
  waiting for transfers between devices: 1240 us -> 1280 us
    all_gather x0 -> x1, waiting for transfers between devices: none -> 142 us  [shards(): grad_n2 = jnp.sum(lax.all_gather(grad_a2, 'tensor'), axis=0)]
    psum x1 -> x0, waiting for transfers between devices: 107 us -> none  [shards(): grad_n2 = lax.psum(grad_a2, 'tensor')]
  transfers between devices with their start and end apart: 14 -> 14, of which waited for: 10 -> 10; matrix products, arithmetic and copies ran while one was open for 11% -> 12% of each run, Pallas kernels for 0% -> 0%
where the time goes in v1:
time: 1700 us
  waiting for transfers between devices  1280 us (75%)
  matrix products  149 us (9%)
  blocking collectives  136 us (8%)
  other arithmetic  77.8 us (5%)
  local copies, waits for them, and re-layouts  38.1 us (2%)
    reduce_scatter x1, waiting for transfers between devices, shards(): lax.psum_scatter(g_w_up, ('dp', 'seq'), scatter_dimension=0, tiled=True)  283 us
    reduce_scatter x1, waiting for transfers between devices, shards(): lax.psum_scatter(g_w_down, ('dp', 'seq'), scatter_dimension=1, tiled=True)  279 us
    all_gather x1, waiting for transfers between devices, shards(): grad_n2 = jnp.sum(lax.all_gather(grad_a2, 'tensor'), axis=0)  142 us
    reduce_scatter x1, waiting for transfers between devices, shards(): lax.psum_scatter(g_w_kv, ('dp', 'seq', 'tensor'), scatter_dimension=0, ti...  140 us
    unnamed x2, blocking collectives  136 us
    psum x1, waiting for transfers between devices, shards(): residual = x_float + (lax.psum(attn_part, 'tensor') + b_out)  118 us
    unnamed x17, waiting for transfers between devices  105 us
    reduce_scatter x1, waiting for transfers between devices, shards(): lax.psum_scatter(g_w_query, ('dp', 'seq'), scatter_dimension=0, tiled=True)  92.1 us
  transfers between devices with their start and end apart: 14, of which 10 were waited for; matrix products, arithmetic and copies ran while one was open for 12% of the time, Pallas kernels for 0%

profile of v1, /device:TPU:0, one launch (start us, length us, event | category | flops | bytes accessed | tf_op | source)
XLA Modules:
  0.0 1696.2 jit_solution(16362376040651974152)
XLA Ops:
  30.5 29.8 %all-gather.4.cloned.1.call-done = bf16[3,1024,256]{2,1,0:T(8,128)(2,1)} async-done(((bf16[3,256,256]{2,1,0:T(8,128)(2,1)}), bf16[3,1024,256]{2,1,0:T(8,128)(2,1)}) %all-gather.4.cloned.1.call-update) | async-done | bytes 1572880 | tf_op jit(solution)/shard_map/all_gather | solution.py:88
  60.4 7.9 fusion.4
  68.3 7.4 fusion.3
  75.8 6.5 fusion.28
  93.7 117.7 %all-reduce.6.cloned.1.call-done = f32[3,256,2048]{2,1,0:T(8,128)} async-done(((f32[3,256,2048]{2,1,0:T(8,128)}), f32[3,256,2048]{2,1,0:T(8,128)}) %all-reduce.6.cloned.1.call-update) | async-done | bytes 6291472 | tf_op jit(solution)/shard_map/psum | solution.py:114
  224.9 8.5 fusion.49
  233.4 14.9 convert_reduce_fusion.1
  248.4 8.6 fusion.50
  257.0 13.3 convolution_convert_fusion
  270.4 141.7 %all-gather.8.cloned.1.call-done = f32[4,3,256,2048]{3,2,1,0:T(8,128)} async-done(((f32[1,3,256,2048]{3,2,1,0:T(8,128)}), f32[4,3,256,2048]{3,2,1,0:T(8,128)}) %all-gather.8.cloned.1.call-update) | async-done | bytes 25165840 | tf_op jit(solution)/shard_map/all_gather | solution.py:145
  412.1 12.8 reduce_sum.185
  447.0 8.7 fusion
  455.7 6.6 fusion.2
  482.8 10.0 fusion.25
  505.8 96.1 %all-reduce.7 = bf16[3,1024,256]{2,0,1:T(4,128)(2,1)} all-reduce(f32[3,1024,256]{2,0,1:T(4,128)} %copy.69), channel_id=4, replica_groups=mesh['dp'=2,'seq'=4,'tensor'=4] {'seq','tensor'}, use_global_device_ids=true, to_apply=%region_13.14.clone | all-reduce | flops 786432 | bytes 4718592
  609.6 14.2 fusion.45
  623.9 12.6 fusion.51
  654.6 40.0 %all-reduce.2 = f32[128]{0:T(128)S(1)} all-reduce(f32[128]{0:T(128)S(1)} %convert_reduce_fusion.4), channel_id=8, replica_groups=mesh['dp'=2,'seq'=4,'tensor'=4] {'dp','seq','tensor'}, use_global_device_ids=true, to_apply=%region_21.22.clone | all-reduce | flops 128 | bytes 1024
  700.6 104.6 %reduce-scatter.35.cloned.1.call-done = f32[64,6]{1,0:T(8,128)} async-done(((f32[2048,6]{1,0:T(8,128)}), f32[64,6]{1,0:T(8,128)}) %reduce-scatter.35.cloned.1.call-update) | async-done | bytes 1552
  806.5 278.5 %reduce-scatter.29.cloned.1.call-done = f32[2048,256]{1,0:T(8,128)} async-done(((f32[2048,2048]{1,0:T(8,128)}), f32[2048,256]{1,0:T(8,128)}) %reduce-scatter.29.cloned.1.call-update) | async-done | bytes 2097168 | tf_op jit(solution)/shard_map/reduce_scatter | solution.py:209
  1085.1 282.9 %reduce-scatter.27.cloned.1.call-done = f32[256,2048]{1,0:T(8,128)} async-done(((f32[2048,2048]{1,0:T(8,128)}), f32[256,2048]{1,0:T(8,128)}) %reduce-scatter.27.cloned.1.call-update) | async-done | bytes 2097168 | tf_op jit(solution)/shard_map/reduce_scatter | solution.py:207
  1368.0 139.9 %reduce-scatter.23.cloned.1.call-done = f32[64,256]{1,0:T(8,128)} async-done(((f32[2048,256]{1,0:T(8,128)}), f32[64,256]{1,0:T(8,128)}) %reduce-scatter.23.cloned.1.call-update) | async-done | bytes 65552 | tf_op jit(solution)/shard_map/reduce_scatter | solution.py:213
  1507.8 89.4 %reduce-scatter.25.cloned.1.call-done = f32[512,256]{1,0:T(8,128)} async-done(((f32[512,2048]{1,0:T(8,128)}), f32[512,256]{1,0:T(8,128)}) %reduce-scatter.25.cloned.1.call-update) | async-done | bytes 524304 | tf_op jit(solution)/shard_map/reduce_scatter | solution.py:206
  1597.2 92.1 %reduce-scatter.21.cloned.1.call-done = f32[256,512]{1,0:T(8,128)} async-done(((f32[2048,512]{1,0:T(8,128)}), f32[256,512]{1,0:T(8,128)}) %reduce-scatter.21.cloned.1.call-update) | async-done | bytes 524304 | tf_op jit(solution)/shard_map/reduce_scatter | solution.py:204
  (178 shorter events, 135.9 us)
Async XLA Ops:
  7.2 76.0 %copy-start = (bf16[512,2048]{1,0:T(8,128)(2,1)S(1)}, bf16[512,2048]{1,0:T(8,128)(2,1)}, u32[]{:S(2)}) copy-start(bf16[512,2048]{1,0:T(8,128)(2,1)} %param.26) | copy-start | bytes 6291460
  7.2 53.2 %all-gather.4.cloned.1.call-start = ((), (), s32[]{:S(2)}) async-start(), calls=%async_computation.10 | async-start | bytes 1966080 | tf_op jit(solution)/shard_map/all_gather | solution.py:88
  20.5 68.9 %all-gather.6.cloned.1.call-start = ((), (), s32[]{:S(2)}) async-start(), calls=%async_computation.13 | async-start | bytes 3932160 | tf_op jit(solution)/shard_map/all_gather | solution.py:135
  21.2 190.1 %all-reduce.6.cloned.1.call-start = ((), (), s32[]{:S(2)}) async-start(), calls=%async_computation.11 | async-start | bytes 12582912 | tf_op jit(solution)/shard_map/psum | solution.py:114
  21.5 8.2 copy-start.29
  87.7 324.4 %all-gather.8.cloned.1.call-start = ((), (), s32[]{:S(2)}) async-start(), calls=%async_computation.14 | async-start | bytes 31457280 | tf_op jit(solution)/shard_map/all_gather | solution.py:145
  222.2 11.3 copy-start.15
  224.9 8.5 copy-start.14
  248.3 8.6 copy-start.32
  257.0 220.1 %reduce-scatter.17.cloned.1.call-start = ((), (), s32[]{:S(2)}) async-start(), calls=%async_computation.12 | async-start | bytes 3932160 | tf_op jit(solution)/shard_map/reduce_scatter | solution.py:129
  270.3 333.9 %reduce-scatter.19.cloned.1.call-start = ((), (), s32[]{:S(2)}) async-start(), calls=%async_computation.15 | async-start | bytes 3932160 | tf_op jit(solution)/shard_map/reduce_scatter | solution.py:187
  455.7 9.3 copy-start.10
  474.8 178.4 %reduce-scatter.33.cloned.1.call-start = ((), (), s32[]{:S(2)}) async-start(), calls=%async_computation.22 | async-start | bytes 73728
  476.9 218.3 %reduce-scatter.31.cloned.1.call-start = ((), (), s32[]{:S(2)}) async-start(), calls=%async_computation.21 | async-start | bytes 73728
  480.3 12.5 slice-start
  482.8 10.0 slice-start.1
  482.8 10.0 copy-start.7
  500.8 103.5 %copy-start.19 = (f32[2048]{0:T(1024)S(1)}, f32[2048]{0:T(1024)}, u32[]{:S(2)}) copy-start(f32[2048]{0:T(1024)} %copy-done.18) | copy-start | bytes 24580
  604.2 200.9 %reduce-scatter.35.cloned.1.call-start = ((), (), s32[]{:S(2)}) async-start(), calls=%async_computation.23 | async-start | bytes 1081344
  609.5 475.5 %reduce-scatter.29.cloned.1.call-start = ((), (), s32[]{:S(2)}) async-start(), calls=%async_computation.20 | async-start | bytes 18874368 | tf_op jit(solution)/shard_map/reduce_scatter | solution.py:209
  623.8 744.1 %reduce-scatter.27.cloned.1.call-start = ((), (), s32[]{:S(2)}) async-start(), calls=%async_computation.19 | async-start | bytes 18874368 | tf_op jit(solution)/shard_map/reduce_scatter | solution.py:207
  636.5 871.4 %reduce-scatter.23.cloned.1.call-start = ((), (), s32[]{:S(2)}) async-start(), calls=%async_computation.17 | async-start | bytes 2162688 | tf_op jit(solution)/shard_map/reduce_scatter | solution.py:213
  639.7 957.5 %reduce-scatter.25.cloned.1.call-start = ((), (), s32[]{:S(2)}) async-start(), calls=%async_computation.18 | async-start | bytes 4718592 | tf_op jit(solution)/shard_map/reduce_scatter | solution.py:206
  647.3 1042.0 %reduce-scatter.21.cloned.1.call-start = ((), (), s32[]{:S(2)}) async-start(), calls=%async_computation.16 | async-start | bytes 4718592 | tf_op jit(solution)/shard_map/reduce_scatter | solution.py:204
  (27 other events, 134.9 us)
Sparse Core Ops, SparseCore 0:
  20.6 39.7 all-gather.3
  61.9 27.4 all-gather.5
  91.8 119.5 all-reduce.5
  257.1 154.9 all-gather.7
  414.5 37.7 reduce-scatter.16
  474.9 38.4 reduce-scatter.18
  516.8 62.4 reduce-scatter.32
  604.3 62.7 reduce-scatter.30
  669.4 135.6 reduce-scatter.34
  809.3 275.6 reduce-scatter.28
  1089.4 278.5 reduce-scatter.26
  1370.7 137.1 reduce-scatter.22
  1512.0 85.1 reduce-scatter.24
  1601.3 87.9 reduce-scatter.20
